TPU v7x, 256 devices: a whole 4x4x8 slice. The times are simulated.
256 devices in a mesh: island: 4 (over z_hi, core), tensor: 64 (over y, x, z_lo).
Axes of the slice: x: 4, y: 4, z: 8 (z_hi: 2, z_lo: 4; z = z_hi * 4 + z_lo), core: 2. Of those that a mesh axis runs over, the one named last changes fastest.
Arguments:
- activations: bfloat16 [4, 1024, 5120], P('island', 'tensor'), may hold values from -30 to 30, as said below
- cotangent: bfloat16 [4, 1024, 5120], P('island', 'tensor'), may hold values from -24 to 24
- gate_weight: bfloat16 [4, 6912, 5120], P('island', 'tensor'), may hold values from -6 to 6
- up_weight: bfloat16 [4, 6912, 5120], P('island', 'tensor'), may hold values from -6 to 6
- down_weight: bfloat16 [4, 6912, 5120], P('island', 'tensor'), may hold values from -6 to 6
- gate_control: bfloat16 [4, 6912, 5120], P('island', 'tensor'), may hold values from -4 to 4
- up_control: bfloat16 [4, 6912, 5120], P('island', 'tensor'), may hold values from -4 to 4
- down_control: bfloat16 [4, 6912, 5120], P('island', 'tensor'), may hold values from -4 to 4
Outputs:
- gate_new: bfloat16 [6912, 5120], P('tensor')
- up_new: bfloat16 [6912, 5120], P('tensor')
- down_new: bfloat16 [6912, 5120], P('tensor')
- gate_control_new: bfloat16 [4, 6912, 5120], P('island', 'tensor')
- up_control_new: bfloat16 [4, 6912, 5120], P('island', 'tensor')
- down_control_new: bfloat16 [4, 6912, 5120], P('island', 'tensor')
Inputs may be any that keep to these rules, and one draw needn't show every extreme that they name: `activations`: real values; columns and tokens carry different scales.
All inputs are finite; a program needn't handle non-finite values.
Results may differ from a plain program's by a relative error of at most 0.0095.
Values may be sent and summed in bfloat16 or wider, within the bound.
No kernel may reach another device: no remote copies, remote signals or barrier semaphores. Data moves between devices by JAX's collectives and lax.ppermute only.
A program may use at most 128 MiB of HBM per device.

v0:
```python
import jax
import jax.numpy as jnp
from jax import lax
from jax.sharding import PartitionSpec as P

D = 5120
FF = 6912
EPSILON = 1e-06
STEP_SIZE = 1.0
PROX_PROB = 0.5


def contract_first(left, right):
    return lax.dot_general(
        left, right, (((0,), (0,)), ((), ())), preferred_element_type=jnp.float32
    )


def contract_last(left, right):
    return lax.dot_general(
        left, right, (((1,), (1,)), ((), ())), preferred_element_type=jnp.float32
    )


def normalize(rows):
    wide = rows.astype(jnp.float32)
    mean_square = jnp.mean(wide * wide, axis=-1, keepdims=True)
    return (wide * lax.rsqrt(mean_square + EPSILON)).astype(jnp.bfloat16)


def block_grads(normed, cot_rows, gate_w, up_w, down_w):
    d_scale = D ** (-0.5)
    f_scale = FF ** (-0.5)
    gate_proj = contract_last(normed, gate_w) * d_scale
    up_proj = contract_last(normed, up_w) * d_scale
    sigmoid_gate = jax.nn.sigmoid(gate_proj)
    activated = gate_proj * sigmoid_gate
    hidden = (activated * up_proj).astype(jnp.bfloat16)
    grad_down = contract_first(hidden, cot_rows) * f_scale
    grad_hidden = contract_last(cot_rows, down_w) * f_scale
    grad_gatepre = (
        grad_hidden * up_proj * sigmoid_gate * (1.0 + gate_proj * (1.0 - sigmoid_gate))
    ).astype(jnp.bfloat16)
    grad_uppre = (grad_hidden * activated).astype(jnp.bfloat16)
    grad_gate = contract_first(grad_gatepre, normed) * d_scale
    grad_up = contract_first(grad_uppre, normed) * d_scale
    return (grad_gate, grad_up, grad_down)


def prox_parts(weight, control, grad):
    control_wide = control.astype(jnp.float32)
    local = weight.astype(jnp.float32) - STEP_SIZE * (grad - control_wide)
    return (local, (local - STEP_SIZE / PROX_PROB * control_wide).astype(jnp.bfloat16))


def fresh_control(control, mean_rounded, local):
    wide = control.astype(jnp.float32) + PROX_PROB / STEP_SIZE * (
        mean_rounded.astype(jnp.float32) - local
    )
    return wide.astype(jnp.bfloat16)[None]


def per_device(
    activations,
    cotangent,
    gate_weight,
    up_weight,
    down_weight,
    gate_control,
    up_control,
    down_control,
):
    own_rows = activations[0]
    own_cot = cotangent[0]
    normed = lax.all_gather(normalize(own_rows), "tensor", axis=0, tiled=True)
    whole_cot = lax.all_gather(own_cot, "tensor", axis=0, tiled=True)
    grad_gate, grad_up, grad_down = block_grads(
        normed, whole_cot, gate_weight[0], up_weight[0], down_weight[0]
    )
    local_gate, term_gate = prox_parts(gate_weight[0], gate_control[0], grad_gate)
    local_up, term_up = prox_parts(up_weight[0], up_control[0], grad_up)
    local_down, term_down = prox_parts(down_weight[0], down_control[0], grad_down)
    count = lax.axis_size("island")
    total_gate, total_up, total_down = (
        lax.psum(term_gate, "island").astype(jnp.float32),
        lax.psum(term_up, "island").astype(jnp.float32),
        lax.psum(term_down, "island").astype(jnp.float32),
    )
    mean_gate = (total_gate / count).astype(jnp.bfloat16)
    mean_up = (total_up / count).astype(jnp.bfloat16)
    mean_down = (total_down / count).astype(jnp.bfloat16)
    new_gate_control = fresh_control(gate_control[0], mean_gate, local_gate)
    new_up_control = fresh_control(up_control[0], mean_up, local_up)
    new_down_control = fresh_control(down_control[0], mean_down, local_down)
    return (mean_gate, mean_up, mean_down, new_gate_control, new_up_control, new_down_control)


def solution(mesh):
    placed = (
        P("island", "tensor", None),
        P("island", "tensor", None),
        P("island", "tensor", None),
        P("island", "tensor", None),
        P("island", "tensor", None),
        P("island", "tensor", None),
        P("island", "tensor", None),
        P("island", "tensor", None),
    )
    return jax.shard_map(
        per_device,
        mesh=mesh,
        in_specs=placed,
        out_specs=(
            P("tensor", None),
            P("tensor", None),
            P("tensor", None),
            P("island", "tensor", None),
            P("island", "tensor", None),
            P("island", "tensor", None),
        ),
        check_vma=False,
    )
```

profile of v0, /device:TPU:1, one launch (start us, length us, event | category | flops | bytes accessed | tf_op | source)
XLA Modules:
  0.0 956.3 jit_solution(8239383202195098988)
XLA Ops:
  7.2 0.0 all-gather.4.cloned.1.call-start
  7.2 1.1 fusion.36
  8.3 1.7 fusion.37
  10.0 0.0 all-gather.4.cloned.1.call-update
  10.0 0.0 all-gather.6.cloned.1.call-start
  10.0 0.7 all-gather.6.cloned.1.call-update
  10.8 0.0 copy-start.11
  10.8 0.0 all-reduce.3.cloned.1.call-start
  10.8 343.7 %all-gather.4.cloned.1.call-done = bf16[1024,5120]{1,0:T(8,128)(2,1)} async-done(((bf16[16,5120]{1,0:T(8,128)(2,1)}), bf16[1024,5120]{1,0:T(8,128)(2,1)}) %all-gather.4.cloned.1.call-update) | async-done | bytes 10485776 | tf_op jit(solution)/shard_map/all_gather | solution.py:75
  354.5 7.9 convolution_multiply_fusion.2
  362.4 0.0 copy-start.8
  362.4 3.5 convolution_multiply_fusion.3
  366.0 367.8 %all-gather.6.cloned.1.call-done = bf16[1,1024,5120]{2,1,0:T(8,128)(2,1)} async-done(((bf16[1,16,5120]{2,1,0:T(8,128)(2,1)}), bf16[1,1024,5120]{2,1,0:T(8,128)(2,1)}) %all-gather.6.cloned.1.call-update) | async-done | bytes 10485776 | tf_op jit(solution)/shard_map/all_gather | solution.py:76
  733.8 7.6 fusion.26
  741.4 0.0 copy-start.2
  741.4 7.5 fusion.24
  749.0 0.0 copy-start.4
  749.0 4.4 fusion.18
  753.4 4.5 fusion.21
  757.8 0.0 all-reduce.3.cloned.1.call-update
  757.9 184.1 %all-reduce.3.cloned.1.call-done = (bf16[108,5120]{1,0:T(8,128)(2,1)}, bf16[108,5120]{1,0:T(8,128)(2,1)}, bf16[108,5120]{1,0:T(8,128)(2,1)}) async-done(((bf16[108,5120]{1,0:T(8,128)(2,1)}, bf16[108,5120]{1,0:T(8,128)(2,1)}, bf16[108,5120]{1,0:T(8,128)(2,1)}), (bf16[108,5120]{1,0:T(8,128)(2,1)}, bf16[108,5120]{1,0:T(8,128)(2,1)}, bf16[108,5120]{1,0:T(8,128)(2,1)})) %all-reduce.3.cloned.1.call-update) | async-done | bytes 3317776 | tf_op jit(solution)/shard_map/psum | solution.py:85
  942.0 4.0 fusion.31
  946.0 0.7 copy-done.14
  946.8 3.0 fusion.29
  (33 shorter events, 0.1 us)
Async XLA Ops:
  7.2 347.3 %all-gather.4.cloned.1.call-start = ((), (), s32[]{:S(2)}) async-start(), calls=%async_computation | async-start | bytes 10649600 | tf_op jit(solution)/shard_map/all_gather | solution.py:75
  10.0 723.7 %all-gather.6.cloned.1.call-start = ((), (), s32[]{:S(2)}) async-start(), calls=%async_computation.1 | async-start | bytes 10649600 | tf_op jit(solution)/shard_map/all_gather | solution.py:76
  10.8 351.7 %copy-start.11 = (bf16[1,108,5120]{2,1,0:T(8,128)(2,1)S(1)}, bf16[1,108,5120]{2,1,0:T(8,128)(2,1)}, u32[]{:S(2)}) copy-start(bf16[1,108,5120]{2,1,0:T(8,128)(2,1)} %param.11) | copy-start | bytes 3317764
  10.8 931.2 %all-reduce.3.cloned.1.call-start = ((), (), s32[]{:S(2)}) async-start(), calls=%async_computation.2 | async-start | bytes 6881280 | tf_op jit(solution)/shard_map/psum | solution.py:85
  354.5 7.9 copy-start
  362.4 371.3 %copy-start.8 = (bf16[1,108,5120]{2,1,0:T(8,128)(2,1)S(1)}, bf16[1,108,5120]{2,1,0:T(8,128)(2,1)}, u32[]{:S(2)}) copy-start(bf16[1,108,5120]{2,1,0:T(8,128)(2,1)} %param.12) | copy-start | bytes 3317764
  733.7 7.6 copy-start.6
  733.7 7.7 copy-start.9
  733.7 15.2 %slice-start = ((s8[10485760]{0:T(1024)(128)(4,1)}), s8[4194304]{0:T(1024)(128)(4,1)S(1)}, s32[]{:S(2)}) async-start(s8[10485760]{0:T(1024)(128)(4,1)} %bitcast.56), calls=%async_computation.3 | async-start | bytes 8388608
  733.8 15.2 %slice-start.1 = ((s8[10485760]{0:T(1024)(128)(4,1)}), s8[4194304]{0:T(1024)(128)(4,1)S(1)}, s32[]{:S(2)}) async-start(s8[10485760]{0:T(1024)(128)(4,1)} %bitcast.56), calls=%async_computation.4 | async-start | bytes 8388608
  741.4 7.5 slice-start.2
  741.4 7.5 copy-start.2
  741.4 7.5 copy-start.10
  749.0 4.4 copy-start.4
  749.0 4.4 copy-start.12
  757.8 184.1 %copy-start.3 = (bf16[1,108,5120]{2,1,0:T(8,128)(2,1)S(1)}, bf16[1,108,5120]{2,1,0:T(8,128)(2,1)}, u32[]{:S(2)}) copy-start(bf16[1,108,5120]{2,1,0:T(8,128)(2,1)} %param.13) | copy-start | bytes 3317764
  941.9 4.1 copy-start.1
  941.9 4.1 copy-start.5
  942.0 4.1 copy-start.7
  942.0 4.1 copy-start.13
  942.0 4.8 copy-start.14
Sparse Core Ops, SparseCore 0:
  10.3 344.1 all-gather.3
  356.3 377.4 all-gather.5
  758.0 183.9 all-reduce.2
where the time goes:
time: 956 us
  waiting for transfers between devices  896 us (94%)
  matrix products  35.3 us (4%)
  between operations  13.9 us (1%)
  other arithmetic  9.76 us (1%)
    all_gather x1, waiting for transfers between devices, per_device(): whole_cot = lax.all_gather(own_cot, 'tensor', axis=0, tiled=True)  368 us
    all_gather x1, waiting for transfers between devices, per_device(): normed = lax.all_gather(normalize(own_rows), 'tensor', axis=0, tiled=True)  344 us
    psum x1, waiting for transfers between devices, per_device(): lax.psum(term_gate, 'island').astype(jnp.float32)  184 us
  transfers between devices with their start and end apart: 3, of which 3 were waited for; matrix products, arithmetic and copies ran while one was open for 1% of the time, Pallas kernels for 0%

commit v1 on v0

--- a/solution.py
+++ b/solution.py
@@ -72,7 +72,13 @@
 ):
     own_rows = activations[0]
     own_cot = cotangent[0]
-    normed = lax.all_gather(normalize(own_rows), "tensor", axis=0, tiled=True)
+    a0 = normalize(own_rows)
+    normed = jnp.concatenate(
+        lax.all_to_all(
+            jnp.stack(tuple((a0 for _ in range(lax.axis_size("tensor")))), 0), "tensor", 0, 0
+        ),
+        0,
+    )
     whole_cot = lax.all_gather(own_cot, "tensor", axis=0, tiled=True)
     grad_gate, grad_up, grad_down = block_grads(
         normed, whole_cot, gate_weight[0], up_weight[0], down_weight[0]

time: 956 us -> 701 us (0.73)
  waiting for transfers between devices: 896 us -> 615 us
  starting transfers between devices: 0.12 us -> 13 us
    all_to_all x0 -> x1, waiting for transfers between devices: none -> 410 us  [per_device(): lax.all_to_all(jnp.stack(tuple((a0 for _ in range(lax.axis_size('tensor')...]
    all_gather x1 -> x0, waiting for transfers between devices: 344 us -> none  [per_device(): normed = lax.all_gather(normalize(own_rows), 'tensor', axis=0, tiled=True)]
    all_gather x1, waiting for transfers between devices: 368 us -> 35.9 us  [per_device(): whole_cot = lax.all_gather(own_cot, 'tensor', axis=0, tiled=True)]
    psum x1, waiting for transfers between devices: 184 us -> 169 us  [per_device(): lax.psum(term_gate, 'island').astype(jnp.float32)]
    all_to_all x0 -> x1, starting transfers between devices: none -> 12.9 us  [per_device(): lax.all_to_all(jnp.stack(tuple((a0 for _ in range(lax.axis_size('tensor')...]
  transfers between devices with their start and end apart: 3 -> 3, of which waited for: 3 -> 3; matrix products, arithmetic and copies ran while one was open for 1% -> 2% of each run, Pallas kernels for 0% -> 0%
where the time goes in v1:
time: 701 us
  waiting for transfers between devices  615 us (88%)
  matrix products  43.1 us (6%)
  between operations  14.2 us (2%)
  starting transfers between devices  13 us (2%)
  other arithmetic  9.1 us (1%)
    all_to_all x1, waiting for transfers between devices, per_device(): lax.all_to_all(jnp.stack(tuple((a0 for _ in range(lax.axis_size('tensor')...  410 us
    psum x1, waiting for transfers between devices, per_device(): lax.psum(term_gate, 'island').astype(jnp.float32)  169 us
    all_gather x1, waiting for transfers between devices, per_device(): whole_cot = lax.all_gather(own_cot, 'tensor', axis=0, tiled=True)  35.9 us
    dot_general x3, matrix products, contract_last(): lax.dot_general(left, right, (((1,), (1,)), ((), ())), preferred_element_...  22.8 us
    dot_general x3, matrix products, contract_first(): lax.dot_general(left, right, (((0,), (0,)), ((), ())), preferred_element_...  20.3 us
  transfers between devices with their start and end apart: 3, of which 3 were waited for; matrix products, arithmetic and copies ran while one was open for 2% of the time, Pallas kernels for 0%

profile of v1, /device:TPU:1, one launch (start us, length us, event | category | flops | bytes accessed | tf_op | source)
XLA Modules:
  0.0 700.7 jit_solution(12630212150312607855)
XLA Ops:
  7.2 1.1 fusion.36
  8.2 1.0 fusion.39
  9.3 5.2 stack.5
  14.5 12.9 %all-to-all-start = ((bf16[64,16,5120]{2,1,0:T(8,128)(2,1)}), bf16[64,16,5120]{2,1,0:T(8,128)(2,1)}, u32[]{:S(2)}, u32[]{:S(2)}) async-start(bf16[64,16,5120]{2,1,0:T(8,128)(2,1)} %stack.5), calls=%async_computation | async-start | bytes 20971520 | tf_op jit(solution)/shard_map/all_to_all | solution.py:77
  27.4 0.0 all-gather.3.cloned.1.call-start
  27.5 0.7 all-gather.3.cloned.1.call-update
  28.2 0.0 all-reduce.3.cloned.1.call-start
  28.2 410.1 %all-to-all-done = bf16[64,16,5120]{2,1,0:T(8,128)(2,1)} async-done(((bf16[64,16,5120]{2,1,0:T(8,128)(2,1)}), bf16[64,16,5120]{2,1,0:T(8,128)(2,1)}, u32[]{:S(2)}, u32[]{:S(2)}) %all-to-all-start) | async-done | bytes 10485792 | tf_op jit(solution)/shard_map/all_to_all | solution.py:77
  438.3 7.6 %convolution_multiply_fusion.2 = f32[1024,108]{0,1:T(8,128)S(1)} fusion(bf16[1024,5120]{1,0:T(8,128)(2,1)} %bitcast.4, bf16[1,108,5120]{2,1,0:T(8,128)(2,1)S(1)} %copy-done.9), kind=kOutput, calls=%fused_computation.31 | convolution fusion | flops 1132572672 | bytes 12034048 | tf_op jit(solution)/shard_map/dot_general | solution.py:20
  445.9 0.0 copy-start.11
  445.9 7.6 %convolution_multiply_fusion.3 = f32[1024,108]{0,1:T(8,128)S(1)} fusion(bf16[1024,5120]{1,0:T(8,128)(2,1)} %bitcast.4, bf16[1,108,5120]{2,1,0:T(8,128)(2,1)S(1)} %copy-done.7), kind=kOutput, calls=%fused_computation.32 | convolution fusion | flops 1132572672 | bytes 12034048 | tf_op jit(solution)/shard_map/dot_general | solution.py:20
  453.5 35.9 %all-gather.3.cloned.1.call-done = bf16[1,1024,5120]{2,1,0:T(8,128)(2,1)} async-done(((bf16[1,16,5120]{2,1,0:T(8,128)(2,1)}), bf16[1,1024,5120]{2,1,0:T(8,128)(2,1)}) %all-gather.3.cloned.1.call-update) | async-done | bytes 10485776 | tf_op jit(solution)/shard_map/all_gather | solution.py:82
  489.4 7.6 %fusion.26 = f32[1024,108]{0,1:T(8,128)S(1)} fusion(bf16[1,1024,5120]{2,1,0:T(8,128)(2,1)} %all-gather.3.cloned.1.call-done, bf16[1,108,5120]{2,1,0:T(8,128)(2,1)S(1)} %copy-done.11), kind=kOutput, calls=%fused_computation.33 | convolution fusion | flops 1132572672 | bytes 12034048 | tf_op jit(solution)/shard_map/dot_general | solution.py:20
  497.1 0.0 copy-start.1
  497.1 0.0 copy-start.10
  497.1 7.5 %fusion.21 = (bf16[108,5120]{1,0:T(8,128)(2,1)}, f32[108,5120]{1,0:T(8,128)S(1)}) fusion(bf16[1,108,5120]{2,1,0:T(8,128)(2,1)S(1)} %copy-done.3, bf16[1024,5120]{1,0:T(8,128)(2,1)} %bitcast.4, f32[1024,108]{0,1:T(8,128)S(1)} %fusion.26, f32[1024,108]{0,1:T(8,128)S(1)} %convolution_multiply_fusion.2, bf16[1,108,5120]{2,1,0:T(8,128)(2,1)S(1)} %copy-done.8), kind=kOutput, calls=%fused_computation.23 | convolution fusion | flops 1137549312 | bytes 16900096 | tf_op jit(solution)/shard_map/dot_general | solution.py:14
  504.6 0.0 copy-start.12
  504.6 8.3 %fusion.18 = (bf16[108,5120]{1,0:T(8,128)(2,1)}, f32[108,5120]{1,0:T(8,128)}) fusion(bf16[1,108,5120]{2,1,0:T(8,128)(2,1)S(1)} %copy-done.1, bf16[1024,5120]{1,0:T(8,128)(2,1)} %bitcast.4, f32[1024,108]{0,1:T(8,128)S(1)} %convolution_multiply_fusion.2, f32[1024,108]{0,1:T(8,128)S(1)} %fusion.26, f32[1024,108]{0,1:T(8,128)S(1)} %convolution_multiply_fusion.3, ...), kind=kOutput, calls=%fused_computation.20 | convolution fusion | flops 1137991680 | bytes 17342464 | tf_op jit(solution)/shard_map/dot_general | solution.py:14
  513.0 4.5 fusion.24
  517.4 0.0 all-reduce.3.cloned.1.call-update
  517.5 168.6 %all-reduce.3.cloned.1.call-done = (bf16[108,5120]{1,0:T(8,128)(2,1)}, bf16[108,5120]{1,0:T(8,128)(2,1)}, bf16[108,5120]{1,0:T(8,128)(2,1)}) async-done(((bf16[108,5120]{1,0:T(8,128)(2,1)}, bf16[108,5120]{1,0:T(8,128)(2,1)}, bf16[108,5120]{1,0:T(8,128)(2,1)}), (bf16[108,5120]{1,0:T(8,128)(2,1)}, bf16[108,5120]{1,0:T(8,128)(2,1)}, bf16[108,5120]{1,0:T(8,128)(2,1)})) %all-reduce.3.cloned.1.call-update) | async-done | bytes 3317776 | tf_op jit(solution)/shard_map/psum | solution.py:91
  686.1 4.0 fusion.31
  690.1 0.7 copy-done.14
  690.9 3.0 fusion.29
  (33 shorter events, 0.1 us)
Async XLA Ops:
  14.5 423.8 %copy-start.9 = (bf16[1,108,5120]{2,1,0:T(8,128)(2,1)S(1)}, bf16[1,108,5120]{2,1,0:T(8,128)(2,1)}, u32[]{:S(2)}) copy-start(bf16[1,108,5120]{2,1,0:T(8,128)(2,1)} %param.10) | copy-start | bytes 3317764
  14.5 423.8 %all-to-all-start = ((bf16[64,16,5120]{2,1,0:T(8,128)(2,1)}), bf16[64,16,5120]{2,1,0:T(8,128)(2,1)}, u32[]{:S(2)}, u32[]{:S(2)}) async-start(bf16[64,16,5120]{2,1,0:T(8,128)(2,1)} %stack.5), calls=%async_computation | async-start | bytes 20971520 | tf_op jit(solution)/shard_map/all_to_all | solution.py:77
  27.4 462.0 %all-gather.3.cloned.1.call-start = ((), (), s32[]{:S(2)}) async-start(), calls=%async_computation.1 | async-start | bytes 10649600 | tf_op jit(solution)/shard_map/all_gather | solution.py:82
  28.2 657.9 %all-reduce.3.cloned.1.call-start = ((), (), s32[]{:S(2)}) async-start(), calls=%async_computation.2 | async-start | bytes 6881280 | tf_op jit(solution)/shard_map/psum | solution.py:91
  438.3 7.6 %copy-start.7 = (bf16[1,108,5120]{2,1,0:T(8,128)(2,1)S(1)}, bf16[1,108,5120]{2,1,0:T(8,128)(2,1)}, u32[]{:S(2)}) copy-start(bf16[1,108,5120]{2,1,0:T(8,128)(2,1)} %param.11) | copy-start | bytes 3317764
  445.9 43.5 %copy-start.11 = (bf16[1,108,5120]{2,1,0:T(8,128)(2,1)S(1)}, bf16[1,108,5120]{2,1,0:T(8,128)(2,1)}, u32[]{:S(2)}) copy-start(bf16[1,108,5120]{2,1,0:T(8,128)(2,1)} %param.12) | copy-start | bytes 3317764
  489.4 7.6 %copy-start.3 = (bf16[1,108,5120]{2,1,0:T(8,128)(2,1)S(1)}, bf16[1,108,5120]{2,1,0:T(8,128)(2,1)}, u32[]{:S(2)}) copy-start(bf16[1,108,5120]{2,1,0:T(8,128)(2,1)} %param.14) | copy-start | bytes 3317764
  489.4 7.6 %copy-start.8 = (bf16[1,108,5120]{2,1,0:T(8,128)(2,1)S(1)}, bf16[1,108,5120]{2,1,0:T(8,128)(2,1)}, u32[]{:S(2)}) copy-start(bf16[1,108,5120]{2,1,0:T(8,128)(2,1)} %param.11) | copy-start | bytes 3317764
  497.1 7.6 %copy-start.1 = (bf16[1,108,5120]{2,1,0:T(8,128)(2,1)S(1)}, bf16[1,108,5120]{2,1,0:T(8,128)(2,1)}, u32[]{:S(2)}) copy-start(bf16[1,108,5120]{2,1,0:T(8,128)(2,1)} %param.13) | copy-start | bytes 3317764
  497.1 7.5 %copy-start.10 = (bf16[1,108,5120]{2,1,0:T(8,128)(2,1)S(1)}, bf16[1,108,5120]{2,1,0:T(8,128)(2,1)}, u32[]{:S(2)}) copy-start(bf16[1,108,5120]{2,1,0:T(8,128)(2,1)} %param.10) | copy-start | bytes 3317764
  497.1 15.9 %slice-start = ((s8[10485760]{0:T(1024)(128)(4,1)}), s8[4194304]{0:T(1024)(128)(4,1)S(1)}, s32[]{:S(2)}) async-start(s8[10485760]{0:T(1024)(128)(4,1)} %bitcast.55), calls=%async_computation.3 | async-start | bytes 8388608
  497.1 15.9 %slice-start.1 = ((s8[10485760]{0:T(1024)(128)(4,1)}), s8[4194304]{0:T(1024)(128)(4,1)S(1)}, s32[]{:S(2)}) async-start(s8[10485760]{0:T(1024)(128)(4,1)} %bitcast.55), calls=%async_computation.4 | async-start | bytes 8388608
  504.6 8.3 %slice-start.2 = ((s8[10485760]{0:T(1024)(128)(4,1)}), s8[2097152]{0:T(1024)(128)(4,1)S(1)}, s32[]{:S(2)}) async-start(s8[10485760]{0:T(1024)(128)(4,1)} %bitcast.55), calls=%async_computation.5 | async-start | bytes 4194304
  504.6 8.3 %copy-start.5 = (bf16[1,108,5120]{2,1,0:T(8,128)(2,1)S(1)}, bf16[1,108,5120]{2,1,0:T(8,128)(2,1)}, u32[]{:S(2)}) copy-start(bf16[1,108,5120]{2,1,0:T(8,128)(2,1)} %param.15) | copy-start | bytes 3317764
  504.6 8.3 %copy-start.12 = (bf16[1,108,5120]{2,1,0:T(8,128)(2,1)S(1)}, bf16[1,108,5120]{2,1,0:T(8,128)(2,1)}, u32[]{:S(2)}) copy-start(bf16[1,108,5120]{2,1,0:T(8,128)(2,1)} %param.12) | copy-start | bytes 3317764
  517.4 168.6 %copy-start.2 = (bf16[1,108,5120]{2,1,0:T(8,128)(2,1)S(1)}, bf16[1,108,5120]{2,1,0:T(8,128)(2,1)}, u32[]{:S(2)}) copy-start(bf16[1,108,5120]{2,1,0:T(8,128)(2,1)} %param.13) | copy-start | bytes 3317764
  686.1 4.1 copy-start
  686.1 4.1 copy-start.4
  686.1 4.1 copy-start.6
  686.1 4.1 copy-start.13
  686.1 4.8 copy-start.14
Sparse Core Ops, SparseCore 0:
  30.0 459.3 all-gather.2
  517.6 168.4 all-reduce.2
